TPU v7x, 32 devices: a whole 2x2x4 slice. The times are simulated.
32 devices in a mesh: dp: 4 (over x, core), ctx: 4 (over z), tensor: 2 (over y).
Axes of the slice: x: 2, y: 2, z: 4, core: 2. Of those that a mesh axis runs over, the one named last changes fastest.
Arguments:
- inputs: bfloat16 [8192, 768], P(('dp', 'ctx')), may hold values from -6 to 6
- segments: int32 [4, 2048], P('dp', 'ctx'), may hold values from 0 to 7, never falling along the last dimension, each value on 1 to 1536 neighbouring positions
- query_proj: bfloat16 [768, 768], P(None, 'tensor'), may hold values from -0.4375 to 0.4375
- key_proj: bfloat16 [768, 768], P(None, 'tensor'), may hold values from -0.21875 to 0.21875
- value_proj: bfloat16 [768, 768], P(None, 'tensor'), may hold values from -0.21875 to 0.21875
- query_bias: bfloat16 [768], P('tensor'), may hold values from -3 to 3
- value_bias: bfloat16 [768], P('tensor'), may hold values from -0.59765625 to 0.59765625
- output_proj: bfloat16 [768, 768], P('tensor'), may hold values from -0.875 to 0.875
- output_bias: bfloat16 [768], replicated, may hold values from -1.1953125 to 1.1953125
- attn_gain: bfloat16 [768], replicated, may hold values from 0.5 to 1.5
- attn_shift: bfloat16 [768], replicated, may hold values from -1.1953125 to 1.1953125
- expand_proj: bfloat16 [768, 3072], P(None, 'tensor'), may hold values from -0.21875 to 0.21875
- expand_bias: bfloat16 [3072], P('tensor'), may hold values from -3 to 3
- shrink_proj: bfloat16 [3072, 768], P('tensor'), may hold values from -0.109375 to 0.109375
- shrink_bias: bfloat16 [768], replicated, may hold values from -1.1953125 to 1.1953125
- final_gain: bfloat16 [768], replicated, may hold values from 0.5 to 1.5
- final_shift: bfloat16 [768], replicated, may hold values from -1.1953125 to 1.1953125
- cotangent: bfloat16 [8192, 768], P(('dp', 'ctx')), may hold values from -6 to 6
Outputs:
- output: bfloat16 [8192, 768], P(('dp', 'ctx'))
- input_grad: float32 [8192, 768], P(('dp', 'ctx'))
- query_grad: float32 [768, 768], P(None, 'tensor')
- key_grad: float32 [768, 768], P(None, 'tensor')
- value_grad: float32 [768, 768], P(None, 'tensor')
- qbias_grad: float32 [768], P('tensor')
- vbias_grad: float32 [768], P('tensor')
- oproj_grad: float32 [768, 768], P('tensor')
- obias_grad: float32 [768], replicated
- again_grad: float32 [768], replicated
- ashift_grad: float32 [768], replicated
- expand_grad: float32 [768, 3072], P(None, 'tensor')
- ebias_grad: float32 [3072], P('tensor')
- shrink_grad: float32 [3072, 768], P('tensor')
- sbias_grad: float32 [768], replicated
- fgain_grad: float32 [768], replicated
- fshift_grad: float32 [768], replicated
Inputs may be any that keep to these rules, and one draw needn't show every extreme that they name: `segments`: along each sequence the ids never fall; every id from 0 to 7 names one document of the sequence, and one document has 1536 tokens.
All inputs are finite; a program needn't handle non-finite values.
Results may differ from a plain program's by a relative error of at most 0.019.
Values may be sent and summed in bfloat16 or wider, within the bound.
A program may use at most 256 MiB of HBM per device.

v0:
```python
import jax
import jax.numpy as jnp
from jax import lax
from jax.sharding import PartitionSpec as P

HEAD_DIM = 64
norm_eps = 1e-12
masked = -1e30
contract_rows = (((0,), (0,)), ((), ()))
contract_cols = (((1,), (1,)), ((), ()))


def matmul(left, right):
    return jnp.dot(left, right, preferred_element_type=jnp.float32)


def inner_rows(left, right):
    return lax.dot_general(left, right, contract_rows, preferred_element_type=jnp.float32)


def inner_cols(left, right):
    return lax.dot_general(left, right, contract_cols, preferred_element_type=jnp.float32)


def norm_forward(values, gain, shift):
    centred = values - jnp.mean(values, axis=-1, keepdims=True)
    spread = jnp.mean(centred * centred, axis=-1, keepdims=True)
    recip = lax.rsqrt(spread + norm_eps)
    normed = centred * recip
    return (normed * gain + shift, normed, recip)


def norm_backward(upstream, normed, recip, gain):
    scaled = upstream * gain
    centred = (
        scaled
        - jnp.mean(scaled, axis=-1, keepdims=True)
        - normed * jnp.mean(scaled * normed, axis=-1, keepdims=True)
    )
    return (centred * recip, jnp.sum(upstream * normed, axis=0), jnp.sum(upstream, axis=0))


def cross_scores(left, right):
    return inner_cols(left, right)


def spread_apply(weights_in, right):
    return matmul(weights_in, right)


def spread_transpose(weights_in, left):
    return inner_rows(weights_in, left)


def body(
    inputs,
    segments,
    query_proj,
    key_proj,
    value_proj,
    query_bias,
    value_bias,
    output_proj,
    output_bias,
    attn_gain,
    attn_shift,
    expand_proj,
    expand_bias,
    shrink_proj,
    shrink_bias,
    final_gain,
    final_shift,
    cotangent,
):
    head_count = query_proj.shape[1] // HEAD_DIM
    scale = HEAD_DIM ** (-0.5)
    seg_local = segments[0]
    queries = (matmul(inputs, query_proj) + query_bias.astype(jnp.float32)).astype(jnp.bfloat16)
    keys = matmul(inputs, key_proj).astype(jnp.bfloat16)
    values = (matmul(inputs, value_proj) + value_bias.astype(jnp.float32)).astype(jnp.bfloat16)
    all_keys, all_values, key_ids = (
        lax.all_gather(keys, "ctx", axis=0, tiled=True),
        lax.all_gather(values, "ctx", axis=0, tiled=True),
        lax.all_gather(seg_local.astype(jnp.bfloat16), "ctx", axis=0, tiled=True),
    )
    query_segs = seg_local.astype(jnp.float32)
    key_segs = key_ids.astype(jnp.float32)
    same_seg = query_segs[:, None] == key_segs[None, :]

    def split_heads(matrix):
        return jnp.swapaxes(matrix.reshape(matrix.shape[0], head_count, HEAD_DIM), 0, 1)

    def join_heads(stack):
        return jnp.swapaxes(stack, 0, 1).reshape(stack.shape[1], head_count * HEAD_DIM)

    query_heads = split_heads(queries)
    key_heads = split_heads(all_keys)
    value_heads = split_heads(all_values)

    def head_forward(state, triple):
        query_head, key_head, value_head = triple
        scores = cross_scores(query_head, key_head) * scale
        scores = jnp.where(same_seg, scores, masked)
        row_max = jnp.max(scores, axis=1, keepdims=True)
        exp_scores = jnp.where(same_seg, jnp.exp(scores - row_max), 0.0)
        row_sum = jnp.sum(exp_scores, axis=1, keepdims=True)
        attn_probs = (exp_scores / row_sum).astype(jnp.bfloat16)
        mixed = spread_apply(attn_probs, value_head)
        return (state, (mixed, row_max + jnp.log(row_sum)))

    mixed_heads, log_sums = lax.scan(head_forward, None, (query_heads, key_heads, value_heads))[1]
    attended = join_heads(mixed_heads).astype(jnp.bfloat16)
    attn_total = lax.psum(matmul(attended, output_proj).astype(jnp.bfloat16), "tensor").astype(
        jnp.float32
    )
    attn_gain_f = attn_gain.astype(jnp.float32)
    first, first_normed, first_recip = norm_forward(
        inputs.astype(jnp.float32) + attn_total + output_bias.astype(jnp.float32),
        attn_gain_f,
        attn_shift.astype(jnp.float32),
    )
    first_low = first.astype(jnp.bfloat16)
    pre_act = matmul(first_low, expand_proj) + expand_bias.astype(jnp.float32)
    activated, gelu_back = jax.vjp(lambda pre_in: jax.nn.gelu(pre_in, approximate=False), pre_act)
    hidden = activated.astype(jnp.bfloat16)
    feed_total = lax.psum(matmul(hidden, shrink_proj).astype(jnp.bfloat16), "tensor").astype(
        jnp.float32
    )
    second = first + feed_total + shrink_bias.astype(jnp.float32)
    final_gain_f = final_gain.astype(jnp.float32)
    output, second_normed, second_recip = norm_forward(
        second, final_gain_f, final_shift.astype(jnp.float32)
    )
    upstream = cotangent.astype(jnp.float32)
    grad_second, fgain_grad, fshift_grad = norm_backward(
        upstream, second_normed, second_recip, final_gain_f
    )
    sbias_grad = jnp.sum(grad_second, axis=0)
    grad_second_low = grad_second.astype(jnp.bfloat16)
    shrink_grad = inner_rows(hidden, grad_second_low)
    grad_act = inner_cols(grad_second_low, shrink_proj)
    grad_pre = gelu_back(grad_act)[0].astype(jnp.bfloat16)
    ebias_grad = jnp.sum(grad_pre.astype(jnp.float32), axis=0)
    expand_grad = inner_rows(first_low, grad_pre)
    grad_first = grad_second + lax.psum(
        inner_cols(grad_pre, expand_proj).astype(jnp.bfloat16), "tensor"
    ).astype(jnp.float32)
    grad_mix, again_grad, ashift_grad = norm_backward(
        grad_first, first_normed, first_recip, attn_gain_f
    )
    obias_grad = jnp.sum(grad_mix, axis=0)
    grad_mix_low = grad_mix.astype(jnp.bfloat16)
    oproj_grad = inner_rows(attended, grad_mix_low)
    grad_attended = inner_cols(grad_mix_low, output_proj).astype(jnp.bfloat16)
    grad_heads = split_heads(grad_attended)

    def head_backward(state, group):
        query_head, key_head, value_head, grad_head, log_sum = group
        scores = cross_scores(query_head, key_head) * scale
        attn_probs = jnp.where(same_seg, jnp.exp(scores - log_sum), 0.0)
        grad_probs = cross_scores(grad_head, value_head)
        row_dot = jnp.sum(attn_probs * grad_probs, axis=1, keepdims=True)
        grad_scores = (attn_probs * (grad_probs - row_dot)).astype(jnp.bfloat16)
        grad_query = spread_apply(grad_scores, key_head) * scale
        grad_key = spread_transpose(grad_scores, query_head) * scale
        grad_value = spread_transpose(attn_probs.astype(jnp.bfloat16), grad_head)
        return (state, (grad_query, grad_key, grad_value))

    query_back, key_back, value_back = lax.scan(
        head_backward, None, (query_heads, key_heads, value_heads, grad_heads, log_sums)
    )[1]
    grad_queries = join_heads(query_back).astype(jnp.bfloat16)
    key_sum, value_sum = (
        lax.psum_scatter(
            join_heads(key_back).astype(jnp.bfloat16), "ctx", scatter_dimension=0, tiled=True
        ).astype(jnp.float32),
        lax.psum_scatter(
            join_heads(value_back).astype(jnp.bfloat16), "ctx", scatter_dimension=0, tiled=True
        ).astype(jnp.float32),
    )
    grad_keys = key_sum.astype(jnp.bfloat16)
    grad_values = value_sum.astype(jnp.bfloat16)
    qbias_grad = jnp.sum(grad_queries.astype(jnp.float32), axis=0)
    vbias_grad = jnp.sum(grad_values.astype(jnp.float32), axis=0)
    query_grad = inner_rows(inputs, grad_queries)
    key_grad = inner_rows(inputs, grad_keys)
    value_grad = inner_rows(inputs, grad_values)
    back_terms = (
        inner_cols(grad_queries, query_proj)
        + inner_cols(grad_keys, key_proj)
        + inner_cols(grad_values, value_proj)
    )
    input_grad = grad_mix + lax.psum(back_terms.astype(jnp.bfloat16), "tensor").astype(jnp.float32)
    (
        query_grad,
        key_grad,
        value_grad,
        qbias_grad,
        vbias_grad,
        oproj_grad,
        obias_grad,
        again_grad,
        ashift_grad,
        expand_grad,
        ebias_grad,
        shrink_grad,
        sbias_grad,
        fgain_grad,
        fshift_grad,
    ) = lax.psum(
        (
            query_grad,
            key_grad,
            value_grad,
            qbias_grad,
            vbias_grad,
            oproj_grad,
            obias_grad,
            again_grad,
            ashift_grad,
            expand_grad,
            ebias_grad,
            shrink_grad,
            sbias_grad,
            fgain_grad,
            fshift_grad,
        ),
        ("dp", "ctx"),
    )
    return (
        output.astype(jnp.bfloat16),
        input_grad,
        query_grad,
        key_grad,
        value_grad,
        qbias_grad,
        vbias_grad,
        oproj_grad,
        obias_grad,
        again_grad,
        ashift_grad,
        expand_grad,
        ebias_grad,
        shrink_grad,
        sbias_grad,
        fgain_grad,
        fshift_grad,
    )


def solution(mesh):
    in_specs = (
        P(("dp", "ctx"), None),
        P("dp", "ctx"),
        P(None, "tensor"),
        P(None, "tensor"),
        P(None, "tensor"),
        P("tensor"),
        P("tensor"),
        P("tensor", None),
        P(),
        P(),
        P(),
        P(None, "tensor"),
        P("tensor"),
        P("tensor", None),
        P(),
        P(),
        P(),
        P(("dp", "ctx"), None),
    )
    out_specs = (
        P(("dp", "ctx"), None),
        P(("dp", "ctx"), None),
        P(None, "tensor"),
        P(None, "tensor"),
        P(None, "tensor"),
        P("tensor"),
        P("tensor"),
        P("tensor", None),
        P(),
        P(),
        P(),
        P(None, "tensor"),
        P("tensor"),
        P("tensor", None),
        P(),
        P(),
        P(),
    )
    return jax.shard_map(body, mesh=mesh, in_specs=in_specs, out_specs=out_specs, check_vma=False)
```

profile of v0, /device:TPU:0, one launch (start us, length us, event | category | flops | bytes accessed | tf_op | source)
XLA Modules:
  0.0 743.4 jit_solution(2113761524882374570)
XLA Ops:
  7.3 2.8 convolution_convert_fusion.4
  10.2 2.4 fusion.62
  12.7 13.7 %all-gather = bf16[1,2048]{1,0:T(2,128)(2,1)S(1)} all-gather(bf16[1,512]{1,0:T(2,128)(2,1)S(1)} %get-tuple-element.288), channel_id=2, replica_groups=mesh['dp'=4,'ctx'=4,'tensor'=2] {'ctx'}, dimensions={1}, use_global_device_ids=true | all-gather | bytes 5120 | tf_op jit(solution)/shard_map/all_gather | solution.py:84
  29.1 21.0 %all-gather.4.cloned.1.call-done = bf16[2048,384]{1,0:T(8,128)(2,1)} async-done(((bf16[512,384]{1,0:T(8,128)(2,1)}), bf16[2048,384]{1,0:T(8,128)(2,1)}) %all-gather.4.cloned.1.call-update) | async-done | bytes 1572880 | tf_op jit(solution)/shard_map/all_gather | solution.py:82
  50.1 2.6 copy.43
  52.6 4.1 copy.45
  56.8 31.5 %all-gather.6.cloned.1.call-done = bf16[2048,384]{1,0:T(8,128)(2,1)} async-done(((bf16[512,384]{1,0:T(8,128)(2,1)}), bf16[2048,384]{1,0:T(8,128)(2,1)}) %all-gather.6.cloned.1.call-update) | async-done | bytes 1572880 | tf_op jit(solution)/shard_map/all_gather | solution.py:83
  88.2 2.6 copy.44
  90.8 4.1 copy.46
  94.9 38.4 %while.28 = (s32[]{:T(128)}, bf16[6,512,64]{1,2,0:T(8,128)(2,1)S(1)}, f32[6,512,1]{1,2,0:T(1,128)}, bf16[6,512,64]{2,1,0:T(8,128)(2,1)}, bf16[6,2048,64]{2,1,0:T...) while((s32[]{:T(128)}, ...), condition=%wide.region_3.4_spmd.clone, body=%wide.region_0.3_spmd.clone.sunk | while | flops 286260736 | bytes 13946985 | solution.py:111
  94.9 2.0 fusion.132
  98.1 2.6 fusion.134
  101.3 2.0 fusion.132
  104.5 2.6 fusion.134
  107.7 2.0 fusion.132
  110.9 2.6 fusion.134
  114.1 2.0 fusion.132
  117.3 2.6 fusion.134
  120.5 2.0 fusion.132
  123.7 2.6 fusion.134
  126.9 2.0 fusion.132
  130.1 2.6 fusion.134
  133.3 2.7 convolution_convert_fusion.2
  140.6 28.8 %all-reduce.8.cloned.1.call-done = bf16[512,768]{1,0:T(8,128)(2,1)} async-done(((bf16[512,768]{1,0:T(8,128)(2,1)}), bf16[512,768]{1,0:T(8,128)(2,1)}) %all-reduce.8.cloned.1.call-update) | async-done | bytes 786448 | tf_op jit(solution)/shard_map/psum | solution.py:113
  171.5 9.5 %multiply_convert_fusion.1 = (bf16[512,1536]{1,0:T(8,128)(2,1)S(1)}, f32[512,1536]{1,0:T(8,128)}, f32[512,1536]{1,0:T(8,128)}) fusion(f32[1536]{0:T(1024)S(1)} %copy-done.41, bf16[768,1536]{1,0:T(8,128)(2,1)S(1)} %copy-done, f32[768]{0:T(1024)S(1)} %copy-done.38, f32[768]{0:T(1024)S(1)} %copy-done.23, f32[512]{0:T(512)S(1)} %add_rsqrt_fusion.1, ...), kind=kOutput, calls=%fused_computation.62 | convolution fusion | flops 1263403008 | bytes 11815936 | tf_op jit(solution)/shard_map/dot_general | solution.py:14
  182.3 2.3 convolution_convert_fusion.1
  184.8 34.2 %all-reduce.10.cloned.1.call-done = bf16[512,768]{1,0:T(8,128)(2,1)} async-done(((bf16[512,768]{1,0:T(8,128)(2,1)}), bf16[512,768]{1,0:T(8,128)(2,1)}) %all-reduce.10.cloned.1.call-update) | async-done | bytes 786448 | tf_op jit(solution)/shard_map/psum | solution.py:126
  219.1 2.2 fusion.78
  225.0 2.9 convert_reduce_fusion
  229.1 2.3 convolution_convert_fusion
  231.5 34.4 %all-reduce.12.cloned.1.call-done = bf16[512,768]{1,0:T(8,128)(2,1)} async-done(((bf16[512,768]{1,0:T(8,128)(2,1)}), bf16[512,768]{1,0:T(8,128)(2,1)}) %all-reduce.12.cloned.1.call-update) | async-done | bytes 786448 | tf_op jit(solution)/shard_map/psum | solution.py:145
  265.9 3.5 multiply_reduce_fusion.1
  273.7 70.0 %while.29 = (s32[]{:T(128)}, bf16[6,512,64]{1,2,0:T(8,128)(2,1)S(1)}, bf16[6,2048,64]{1,2,0:T(8,128)(2,1)}, bf16[6,2048,64]{1,2,0:T(8,128)(2,1)}, bf16[6,512,64]...) while((s32[]{:T(128)}, ...), condition=%wide.region_17.18_spmd.clone, body=%wide.region_15.17_spmd.clone.sunk | while | flops 681737728 | bytes 34759808 | solution.py:169
  276.2 2.6 multiply_reduce_fusion.7
  279.3 2.1 fusion.146
  283.2 2.2 fusion.145
  287.9 2.6 multiply_reduce_fusion.7
  290.9 2.2 fusion.146
  294.9 2.1 fusion.145
  299.5 2.6 multiply_reduce_fusion.7
  302.6 2.2 fusion.146
  306.6 2.1 fusion.145
  311.2 2.6 multiply_reduce_fusion.7
  314.3 2.2 fusion.146
  318.2 2.1 fusion.145
  322.9 2.6 multiply_reduce_fusion.7
  325.9 2.2 fusion.146
  329.9 2.1 fusion.145
  334.5 2.6 multiply_reduce_fusion.7
  337.6 2.1 fusion.146
  341.5 2.1 fusion.145
  345.1 5.1 fusion.67
  350.3 3.8 fusion.73
  357.4 21.8 %reduce-scatter.3.cloned.1.call-done = bf16[512,384]{0,1:T(8,128)(2,1)} async-done(((bf16[2048,384]{0,1:T(8,128)(2,1)}), bf16[512,384]{0,1:T(8,128)(2,1)}) %reduce-scatter.3.cloned.1.call-update) | async-done | bytes 393232 | tf_op jit(solution)/shard_map/reduce_scatter | solution.py:174
  379.1 3.0 fusion.82
  382.1 33.8 %reduce-scatter.5.cloned.1.call-done = bf16[512,384]{0,1:T(8,128)(2,1)} async-done(((bf16[2048,384]{0,1:T(8,128)(2,1)}), bf16[512,384]{0,1:T(8,128)(2,1)}) %reduce-scatter.5.cloned.1.call-update) | async-done | bytes 393232 | tf_op jit(solution)/shard_map/reduce_scatter | solution.py:177
  415.8 3.5 add_convert_fusion.1
  424.7 61.2 %all-reduce = (f32[384]{0:T(512)}, f32[384]{0:T(512)}, f32[768]{0:T(1024)}, f32[768]{0:T(1024)}, f32[768]{0:T(1024)}, /*index=5*/f32[1536]{0:T(1024)}, f32[768]{0:T(1024)}, f32[768]{0:T(1024)}, f32[768]{0:T(1024)}) all-reduce(f32[384]{0:T(512)S(1)} %reduce_sum.182, ...), channel_id=1, replica_groups=mesh['dp'=4,'ctx'=4,'tensor'=2] {'dp','ctx'}, use_global_device_ids=true, to_apply=%region_25.26 | all-reduce | flops 6912 | bytes 55296 | tf_op jit(solution)/shard_map/psum | solution.py:210
  485.9 2.4 convert_add_fusion
  488.3 231.7 %all-reduce.16.cloned.1.call-done = (f32[768,384]{0,1:T(8,128)}, f32[768,384]{0,1:T(8,128)}, f32[768,384]{0,1:T(8,128)}, f32[384,768]{1,0:T(8,128)}, f32[768,1536]{1,0:T(8,128)}, /*index=5*/f32[1536,768]{1,0:T(8,128)}) async-done(((f32[768,384]{0,1:T(8,128)}, f32[768,384]{0,1:T(8,128)}, f32[768,384]{0,1:T(8,128)}, f32[384,768]{1,0:T(8,128)}, f32[768,1536]{1,0:T(8,128)}, /*index=5*/f32[1536,768]{1,0:T(8,128)}), ...) | async-done | bytes 14155792 | tf_op jit(solution)/shard_map/psum | solution.py:210
  720.1 2.7 copy.50
  722.8 2.7 copy.51
  728.0 5.5 copy.92
  733.5 2.4 copy.93
  (219 shorter events, 72.9 us)
Async XLA Ops:
  7.2 164.2 %copy-start = (bf16[768,1536]{1,0:T(8,128)(2,1)S(1)}, bf16[768,1536]{1,0:T(8,128)(2,1)}, u32[]{:S(2)}) copy-start(bf16[768,1536]{1,0:T(8,128)(2,1)} %param.33) | copy-start | bytes 7077892
  7.2 3.0 copy-start.2
  7.2 2.9 copy-start.47
  7.2 5.4 copy-start.48
  7.2 5.4 copy-start.43
  7.2 42.8 %all-gather.4.cloned.1.call-start = ((), (), s32[]{:S(2)}) async-start(), calls=%async_computation.2 | async-start | bytes 1966080 | tf_op jit(solution)/shard_map/all_gather | solution.py:82
  10.1 78.1 %all-gather.6.cloned.1.call-start = ((), (), s32[]{:S(2)}) async-start(), calls=%async_computation.3 | async-start | bytes 1966080 | tf_op jit(solution)/shard_map/all_gather | solution.py:83
  12.6 156.8 %all-reduce.8.cloned.1.call-start = ((), (), s32[]{:S(2)}) async-start(), calls=%async_computation.4 | async-start | bytes 1572864 | tf_op jit(solution)/shard_map/psum | solution.py:113
  133.3 38.1 %copy-start.12 = (bf16[6,512,64]{1,2,0:T(8,128)(2,1)}, bf16[6,512,64]{1,2,0:T(8,128)(2,1)S(1)}, u32[]{:S(2)}) copy-start(bf16[6,512,64]{1,2,0:T(8,128)(2,1)S(1)} %get-tuple-element.109) | copy-start | bytes 1179652
  136.0 83.0 %all-reduce.10.cloned.1.call-start = ((), (), s32[]{:S(2)}) async-start(), calls=%async_computation.5 | async-start | bytes 1572864 | tf_op jit(solution)/shard_map/psum | solution.py:126
  169.4 1.6 copy-start.8
  169.4 2.1 copy-start.23
  169.4 2.1 copy-start.38
  169.4 2.1 copy-start.41
  170.9 10.1 %copy-start.26 = (f32[512]{0:T(512)}, f32[512]{0:T(512)S(1)}, u32[]{:S(2)}) copy-start(f32[512]{0:T(512)S(1)} %broadcast_multiply_fusion.5) | copy-start | bytes 6148
  171.5 9.6 %copy-start.29 = (f32[512]{0:T(512)}, f32[512]{0:T(512)S(1)}, u32[]{:S(2)}) copy-start(f32[512]{0:T(512)S(1)} %add_rsqrt_fusion.1) | copy-start | bytes 6148
  171.5 10.7 %copy-start.49 = (bf16[1536,768]{1,0:T(8,128)(2,1)S(1)}, bf16[1536,768]{1,0:T(8,128)(2,1)}, u32[]{:S(2)}) copy-start(bf16[1536,768]{1,0:T(8,128)(2,1)} %param.35) | copy-start | bytes 7077892
  181.0 1.2 copy-start.16
  182.2 2.6 copy-start.44
  182.2 2.6 copy-start.45
  182.2 2.6 copy-start.46
  182.2 36.8 %copy-start.24 = (f32[768]{0:T(1024)S(1)}, f32[768]{0:T(1024)}, u32[]{:S(2)}) copy-start(f32[768]{0:T(1024)} %convert_element_type.185) | copy-start | bytes 9220
  182.2 36.8 %copy-start.27 = (f32[512]{0:T(512)S(1)}, f32[512]{0:T(512)}, u32[]{:S(2)}) copy-start(f32[512]{0:T(512)} %copy-done.26) | copy-start | bytes 6148
  182.2 36.8 %copy-start.30 = (f32[512]{0:T(512)S(1)}, f32[512]{0:T(512)}, u32[]{:S(2)}) copy-start(f32[512]{0:T(512)} %copy-done.29) | copy-start | bytes 6148
  182.2 36.8 %copy-start.39 = (f32[768]{0:T(1024)S(1)}, f32[768]{0:T(1024)}, u32[]{:S(2)}) copy-start(f32[768]{0:T(1024)} %convert_element_type.186) | copy-start | bytes 9220
  184.5 81.4 %all-reduce.12.cloned.1.call-start = ((), (), s32[]{:S(2)}) async-start(), calls=%async_computation.6 | async-start | bytes 1572864 | tf_op jit(solution)/shard_map/psum | solution.py:145
  219.0 2.6 copy-start.14
  221.3 3.4 copy-start.54
  221.6 3.1 copy-start.53
  223.0 2.1 copy-start.50
  224.7 3.2 copy-start.3
  227.9 1.2 copy-start.51
  231.4 38.0 %copy-start.4 = (f32[512,768]{1,0:T(8,128)S(1)}, f32[512,768]{1,0:T(8,128)}, u32[]{:S(2)}) copy-start(f32[512,768]{1,0:T(8,128)} %copy-done.3) | copy-start | bytes 4718596
  231.4 38.0 %copy-start.9 = (bf16[512,768]{1,0:T(8,128)(2,1)S(1)}, bf16[512,768]{1,0:T(8,128)(2,1)}, u32[]{:S(2)}) copy-start(bf16[512,768]{1,0:T(8,128)(2,1)} %all-reduce.8.cloned.1.call-done) | copy-start | bytes 2359300
  231.4 147.7 %reduce-scatter.3.cloned.1.call-start = ((), (), s32[]{:S(2)}) async-start(), calls=%async_computation.7 | async-start | bytes 1966080 | tf_op jit(solution)/shard_map/reduce_scatter | solution.py:174
  265.9 3.6 copy-start.15
  269.5 2.5 copy-start.17
  270.8 1.1 copy-start.6
  343.7 1.4 copy-start.5
  343.7 72.2 %reduce-scatter.5.cloned.1.call-start = ((), (), s32[]{:S(2)}) async-start(), calls=%async_computation.8 | async-start | bytes 1966080 | tf_op jit(solution)/shard_map/reduce_scatter | solution.py:177
  344.4 5.8 copy-start.10
  344.4 5.8 copy-start.25
  344.5 5.8 copy-start.28
  344.5 5.7 copy-start.31
  344.5 141.4 %all-reduce.14.cloned.1.call-start = ((), (), s32[]{:S(2)}) async-start(), calls=%async_computation.9 | async-start | bytes 1572864 | tf_op jit(solution)/shard_map/psum | solution.py:193
  345.1 5.2 copy-start.40
  345.1 5.2 copy-start.52
  350.2 3.9 copy-start.22
  354.1 1.8 copy-start.7
  354.1 1.8 copy-start.13
  357.4 58.5 %copy-start.21 = (bf16[768,384]{1,0:T(8,128)(2,1)S(1)}, bf16[768,384]{1,0:T(8,128)(2,1)}, u32[]{:S(2)}) copy-start(bf16[768,384]{1,0:T(8,128)(2,1)} %param.26) | copy-start | bytes 1769476
  419.4 1.6 copy-start.11
  419.4 3.0 copy-start.18
  419.4 300.7 %all-reduce.16.cloned.1.call-start = ((), (), s32[]{:S(2)}) async-start(), calls=%async_computation.10 | async-start | bytes 28311552 | tf_op jit(solution)/shard_map/psum | solution.py:210
  423.9 0.7 copy-start.34
  423.9 0.7 copy-start.35
  423.9 0.7 copy-start.36
  423.9 0.7 copy-start.37
  423.9 0.7 copy-start.42
  720.1 5.5 copy-start.20
  722.8 4.1 copy-start.19
  727.0 6.5 slice-start
  728.0 5.5 slice-start.1
  733.5 3.4 copy-start.1
  (2 other events, 1.4 us)
Sparse Core Ops, SparseCore 0:
  10.2 39.8 all-gather.3
  52.2 35.9 all-gather.5
  136.1 33.1 all-reduce.7
  184.7 34.3 all-reduce.9
  231.5 34.3 all-reduce.11
  343.8 35.2 reduce-scatter.2
  381.5 34.2 reduce-scatter.4
  419.5 33.2 all-reduce.13
  459.1 260.8 all-reduce.15
where the time goes:
time: 746 us; the launch traced here: 743 us
  waiting for transfers between devices  438 us (59%)
  matrix products  141 us (19%)
  blocking collectives  74.9 us (10%)
  local copies, waits for them, and re-layouts  44.8 us (6%)
  other arithmetic  29.9 us (4%)
  between operations  14.4 us (2%)
    psum x1, waiting for transfers between devices, body(): lax.psum((query_grad, key_grad, value_grad, qbias_grad, vbias_grad, oproj...  232 us
    psum x1, blocking collectives, body(): lax.psum((query_grad, key_grad, value_grad, qbias_grad, vbias_grad, oproj...  61.2 us
    dot_general x24, matrix products, inner_cols(): lax.dot_general(left, right, contract_cols, preferred_element_type=jnp.fl...  52.3 us
    dot_general x18, matrix products, matmul(): return jnp.dot(left, right, preferred_element_type=jnp.float32)  47.6 us
    dot_general x18, matrix products, inner_rows(): lax.dot_general(left, right, contract_rows, preferred_element_type=jnp.fl...  40.7 us
    psum x1, waiting for transfers between devices, body(): lax.psum(inner_cols(grad_pre, expand_proj).astype(jnp.bfloat16), 'tensor')  34.4 us
    psum x1, waiting for transfers between devices, body(): lax.psum(matmul(hidden, shrink_proj).astype(jnp.bfloat16), 'tensor')  34.2 us
    reduce_scatter x1, waiting for transfers between devices, body(): lax.psum_scatter(join_heads(value_back).astype(jnp.bfloat16), 'ctx', scat...  33.8 us
  transfers between devices with their start and end apart: 9, of which 8 were waited for; matrix products, arithmetic and copies ran while one was open for 5% of the time, Pallas kernels for 0%

commit v1 on v0

--- a/solution.py
+++ b/solution.py
@@ -78,9 +78,15 @@
     queries = (matmul(inputs, query_proj) + query_bias.astype(jnp.float32)).astype(jnp.bfloat16)
     keys = matmul(inputs, key_proj).astype(jnp.bfloat16)
     values = (matmul(inputs, value_proj) + value_bias.astype(jnp.float32)).astype(jnp.bfloat16)
+
+    def manage_grid(vec):
+        outer = jax.lax.axis_size("ctx")
+        a_next = jnp.concatenate(outer * [vec], axis=0)
+        return jax.lax.all_to_all(a_next, "ctx", 0, 0, tiled=True)
+
     all_keys, all_values, key_ids = (
         lax.all_gather(keys, "ctx", axis=0, tiled=True),
-        lax.all_gather(values, "ctx", axis=0, tiled=True),
+        manage_grid(values),
         lax.all_gather(seg_local.astype(jnp.bfloat16), "ctx", axis=0, tiled=True),
     )
     query_segs = seg_local.astype(jnp.float32)

time: 746 us -> 759 us (1.017)
  waiting for transfers between devices: 438 us -> 386 us
  blocking collectives: 74.9 us -> 124 us
  local copies, waits for them, and re-layouts: 44.8 us -> 52.8 us
    all_gather x1, blocking collectives: 13.7 us -> 62.5 us  [body(): lax.all_gather(seg_local.astype(jnp.bfloat16), 'ctx', axis=0, tiled=True)]
    all_gather x1 -> x0, waiting for transfers between devices: 31.5 us -> none  [body(): lax.all_gather(values, 'ctx', axis=0, tiled=True)]
    all_gather x1, waiting for transfers between devices: 21 us -> 0.01 us  [body(): lax.all_gather(keys, 'ctx', axis=0, tiled=True)]
    unnamed x122 -> x120, local copies, waits for them, and re-layouts: 29.6 us -> 30 us
  transfers between devices with their start and end apart: 9 -> 9, of which waited for: 8 -> 6; matrix products, arithmetic and copies ran while one was open for 5% -> 6% of each run, Pallas kernels for 0% -> 0%
where the time goes in v1:
time: 759 us; the launch traced here: 757 us
  waiting for transfers between devices  386 us (51%)
  matrix products  140 us (18%)
  blocking collectives  124 us (16%)
  local copies, waits for them, and re-layouts  52.8 us (7%)
  other arithmetic  32 us (4%)
  between operations  14.7 us (2%)
    psum x1, waiting for transfers between devices, body(): lax.psum((query_grad, key_grad, value_grad, qbias_grad, vbias_grad, oproj...  231 us
    all_gather x1, blocking collectives, body(): lax.all_gather(seg_local.astype(jnp.bfloat16), 'ctx', axis=0, tiled=True)  62.5 us
    psum x1, blocking collectives, body(): lax.psum((query_grad, key_grad, value_grad, qbias_grad, vbias_grad, oproj...  61.5 us
    dot_general x24, matrix products, inner_cols(): lax.dot_general(left, right, contract_cols, preferred_element_type=jnp.fl...  52.3 us
    dot_general x18, matrix products, matmul(): return jnp.dot(left, right, preferred_element_type=jnp.float32)  46.6 us
    dot_general x18, matrix products, inner_rows(): lax.dot_general(left, right, contract_rows, preferred_element_type=jnp.fl...  40.7 us
    psum x1, waiting for transfers between devices, body(): lax.psum(matmul(hidden, shrink_proj).astype(jnp.bfloat16), 'tensor')  34.4 us
    psum x1, waiting for transfers between devices, body(): lax.psum(inner_cols(grad_pre, expand_proj).astype(jnp.bfloat16), 'tensor')  34.2 us
  transfers between devices with their start and end apart: 9, of which 6 were waited for; matrix products, arithmetic and copies ran while one was open for 6% of the time, Pallas kernels for 0%

profile of v1, /device:TPU:0, one launch (start us, length us, event | category | flops | bytes accessed | tf_op | source)
XLA Modules:
  0.0 756.7 jit_solution(7866176037499462892)
XLA Ops:
  11.2 2.6 copy.54
  13.8 6.5 all-to-all-start
  20.3 2.4 convolution_convert_fusion.4
  22.8 62.5 %all-gather = bf16[1,2048]{1,0:T(2,128)(2,1)S(1)} all-gather(bf16[1,512]{1,0:T(2,128)(2,1)S(1)} %get-tuple-element.324), channel_id=2, replica_groups=mesh['dp'=4,'ctx'=4,'tensor'=2] {'ctx'}, dimensions={1}, use_global_device_ids=true | all-gather | bytes 5120 | tf_op jit(solution)/shard_map/all_gather | solution.py:90
  88.0 3.8 copy.55
  91.8 3.8 reshape.141
  95.6 4.1 copy.57
  99.7 2.6 copy.53
  102.3 4.1 copy.56
  106.4 38.4 %while.28 = (s32[]{:T(128)}, bf16[6,512,64]{1,2,0:T(8,128)(2,1)S(1)}, f32[6,512,1]{1,2,0:T(1,128)}, bf16[6,512,64]{2,1,0:T(8,128)(2,1)}, bf16[6,2048,64]{2,1,0:T...) while((s32[]{:T(128)}, ...), condition=%wide.region_3.4_spmd.clone, body=%wide.region_0.3_spmd.clone.sunk | while | flops 286260736 | bytes 13946985 | solution.py:117
  106.4 2.0 fusion.132
  109.6 2.6 fusion.134
  112.8 2.0 fusion.132
  116.0 2.6 fusion.134
  119.2 2.0 fusion.132
  122.4 2.6 fusion.134
  125.6 2.0 fusion.132
  128.8 2.6 fusion.134
  132.0 2.0 fusion.132
  135.2 2.6 fusion.134
  138.4 2.0 fusion.132
  141.6 2.6 fusion.134
  144.8 2.7 convolution_convert_fusion.2
  152.3 30.3 %all-reduce.8.cloned.1.call-done = bf16[512,768]{1,0:T(8,128)(2,1)} async-done(((bf16[512,768]{1,0:T(8,128)(2,1)}), bf16[512,768]{1,0:T(8,128)(2,1)}) %all-reduce.8.cloned.1.call-update) | async-done | bytes 786448 | tf_op jit(solution)/shard_map/psum | solution.py:119
  184.6 9.5 %multiply_convert_fusion.1 = (bf16[512,1536]{1,0:T(8,128)(2,1)S(1)}, f32[512,1536]{1,0:T(8,128)}, f32[512,1536]{1,0:T(8,128)}) fusion(f32[1536]{0:T(1024)S(1)} %copy-done.41, bf16[768,1536]{1,0:T(8,128)(2,1)S(1)} %copy-done, f32[768]{0:T(1024)S(1)} %copy-done.38, f32[768]{0:T(1024)S(1)} %copy-done.23, f32[512]{0:T(512)S(1)} %add_rsqrt_fusion.1, ...), kind=kOutput, calls=%fused_computation.62 | convolution fusion | flops 1263403008 | bytes 11815936 | tf_op jit(solution)/shard_map/dot_general | solution.py:14
  195.4 2.3 convolution_convert_fusion.1
  197.8 34.4 %all-reduce.10.cloned.1.call-done = bf16[512,768]{1,0:T(8,128)(2,1)} async-done(((bf16[512,768]{1,0:T(8,128)(2,1)}), bf16[512,768]{1,0:T(8,128)(2,1)}) %all-reduce.10.cloned.1.call-update) | async-done | bytes 786448 | tf_op jit(solution)/shard_map/psum | solution.py:132
  232.2 2.2 fusion.78
  238.1 2.9 convert_reduce_fusion
  242.2 2.3 convolution_convert_fusion
  244.8 34.2 %all-reduce.12.cloned.1.call-done = bf16[512,768]{1,0:T(8,128)(2,1)} async-done(((bf16[512,768]{1,0:T(8,128)(2,1)}), bf16[512,768]{1,0:T(8,128)(2,1)}) %all-reduce.12.cloned.1.call-update) | async-done | bytes 786448 | tf_op jit(solution)/shard_map/psum | solution.py:151
  279.0 3.5 multiply_reduce_fusion.1
  286.8 70.0 %while.29 = (s32[]{:T(128)}, bf16[6,512,64]{1,2,0:T(8,128)(2,1)S(1)}, bf16[6,2048,64]{1,2,0:T(8,128)(2,1)}, bf16[6,2048,64]{1,2,0:T(8,128)(2,1)}, bf16[6,512,64]...) while((s32[]{:T(128)}, ...), condition=%wide.region_17.18_spmd.clone, body=%wide.region_15.17_spmd.clone.sunk | while | flops 681737728 | bytes 34759808 | solution.py:175
  289.3 2.6 multiply_reduce_fusion.7
  292.4 2.2 fusion.146
  296.3 2.1 fusion.145
  301.0 2.6 multiply_reduce_fusion.7
  304.0 2.2 fusion.146
  308.0 2.1 fusion.145
  312.6 2.6 multiply_reduce_fusion.7
  315.7 2.2 fusion.146
  319.6 2.1 fusion.145
  324.3 2.6 multiply_reduce_fusion.7
  327.3 2.2 fusion.146
  331.3 2.1 fusion.145
  335.9 2.6 multiply_reduce_fusion.7
  339.0 2.2 fusion.146
  343.0 2.1 fusion.145
  347.6 2.6 multiply_reduce_fusion.7
  350.7 2.2 fusion.146
  354.6 2.1 fusion.145
  358.2 5.1 fusion.67
  363.4 3.8 fusion.73
  370.5 21.8 %reduce-scatter.3.cloned.1.call-done = bf16[512,384]{0,1:T(8,128)(2,1)} async-done(((bf16[2048,384]{0,1:T(8,128)(2,1)}), bf16[512,384]{0,1:T(8,128)(2,1)}) %reduce-scatter.3.cloned.1.call-update) | async-done | bytes 393232 | tf_op jit(solution)/shard_map/reduce_scatter | solution.py:180
  392.2 3.0 fusion.82
  395.2 33.6 %reduce-scatter.5.cloned.1.call-done = bf16[512,384]{0,1:T(8,128)(2,1)} async-done(((bf16[2048,384]{0,1:T(8,128)(2,1)}), bf16[512,384]{0,1:T(8,128)(2,1)}) %reduce-scatter.5.cloned.1.call-update) | async-done | bytes 393232 | tf_op jit(solution)/shard_map/reduce_scatter | solution.py:183
  428.8 3.5 add_convert_fusion.1
  437.9 61.5 %all-reduce = (f32[384]{0:T(512)}, f32[384]{0:T(512)}, f32[768]{0:T(1024)}, f32[768]{0:T(1024)}, f32[768]{0:T(1024)}, /*index=5*/f32[1536]{0:T(1024)}, f32[768]{0:T(1024)}, f32[768]{0:T(1024)}, f32[768]{0:T(1024)}) all-reduce(f32[384]{0:T(512)S(1)} %reduce_sum.182, ...), channel_id=1, replica_groups=mesh['dp'=4,'ctx'=4,'tensor'=2] {'dp','ctx'}, use_global_device_ids=true, to_apply=%region_25.26 | all-reduce | flops 6912 | bytes 55296 | tf_op jit(solution)/shard_map/psum | solution.py:216
  499.4 2.5 convert_add_fusion
  501.8 231.2 %all-reduce.16.cloned.1.call-done = (f32[768,384]{0,1:T(8,128)}, f32[768,384]{0,1:T(8,128)}, f32[768,384]{0,1:T(8,128)}, f32[384,768]{1,0:T(8,128)}, f32[768,1536]{1,0:T(8,128)}, /*index=5*/f32[1536,768]{1,0:T(8,128)}) async-done(((f32[768,384]{0,1:T(8,128)}, f32[768,384]{0,1:T(8,128)}, f32[768,384]{0,1:T(8,128)}, f32[384,768]{1,0:T(8,128)}, f32[768,1536]{1,0:T(8,128)}, /*index=5*/f32[1536,768]{1,0:T(8,128)}), ...) | async-done | bytes 14155792 | tf_op jit(solution)/shard_map/psum | solution.py:216
  733.0 2.7 copy.61
  735.8 2.7 copy.62
  741.0 5.5 copy.103
  746.5 2.4 copy.104
  (219 shorter events, 77.2 us)
Async XLA Ops:
  7.2 177.4 %copy-start = (bf16[768,1536]{1,0:T(8,128)(2,1)S(1)}, bf16[768,1536]{1,0:T(8,128)(2,1)}, u32[]{:S(2)}) copy-start(bf16[768,1536]{1,0:T(8,128)(2,1)} %param.33) | copy-start | bytes 7077892
  13.8 6.5 copy-start.2
  13.8 8.9 %copy-start.47 = (bf16[384]{0:T(512)(128)(2,1)S(1)}, bf16[384]{0:T(512)(128)(2,1)}, u32[]{:S(2)}) copy-start(bf16[384]{0:T(512)(128)(2,1)} %param.27) | copy-start | bytes 2308
  13.8 9.0 %copy-start.43 = (s32[1,512]{1,0:T(1,128)S(1)}, s32[1,512]{1,0:T(1,128)}, u32[]{:S(2)}) copy-start(s32[1,512]{1,0:T(1,128)} %param.23) | copy-start | bytes 6148
  13.8 74.2 %all-to-all-start = ((bf16[4,512,384]{1,2,0:T(8,128)(2,1)}), bf16[4,512,384]{1,2,0:T(8,128)(2,1)}, u32[]{:S(2)}, u32[]{:S(2)}) async-start(bf16[4,512,384]{1,2,0:T(8,128)(2,1)} %copy.54), calls=%async_computation | async-start | bytes 3145728 | tf_op jit(solution)/shard_map/all_to_all | solution.py:85
  20.2 79.4 %all-gather.3.cloned.1.call-start = ((), (), s32[]{:S(2)}) async-start(), calls=%async_computation.3 | async-start | bytes 1966080 | tf_op jit(solution)/shard_map/all_gather | solution.py:88
  22.7 159.9 %all-reduce.8.cloned.1.call-start = ((), (), s32[]{:S(2)}) async-start(), calls=%async_computation.4 | async-start | bytes 1572864 | tf_op jit(solution)/shard_map/psum | solution.py:119
  144.8 39.7 %copy-start.12 = (bf16[6,512,64]{1,2,0:T(8,128)(2,1)}, bf16[6,512,64]{1,2,0:T(8,128)(2,1)S(1)}, u32[]{:S(2)}) copy-start(bf16[6,512,64]{1,2,0:T(8,128)(2,1)S(1)} %get-tuple-element.109) | copy-start | bytes 1179652
  147.5 84.6 %all-reduce.10.cloned.1.call-start = ((), (), s32[]{:S(2)}) async-start(), calls=%async_computation.5 | async-start | bytes 1572864 | tf_op jit(solution)/shard_map/psum | solution.py:132
  182.5 1.6 copy-start.8
  182.5 2.1 copy-start.23
  182.5 2.1 copy-start.38
  182.5 2.1 copy-start.41
  184.1 10.1 %copy-start.26 = (f32[512]{0:T(512)}, f32[512]{0:T(512)S(1)}, u32[]{:S(2)}) copy-start(f32[512]{0:T(512)S(1)} %broadcast_multiply_fusion.5) | copy-start | bytes 6148
  184.6 9.5 %copy-start.29 = (f32[512]{0:T(512)}, f32[512]{0:T(512)S(1)}, u32[]{:S(2)}) copy-start(f32[512]{0:T(512)S(1)} %add_rsqrt_fusion.1) | copy-start | bytes 6148
  184.6 10.7 %copy-start.48 = (bf16[1536,768]{1,0:T(8,128)(2,1)S(1)}, bf16[1536,768]{1,0:T(8,128)(2,1)}, u32[]{:S(2)}) copy-start(bf16[1536,768]{1,0:T(8,128)(2,1)} %param.35) | copy-start | bytes 7077892
  194.1 1.1 copy-start.16
  195.3 2.4 copy-start.44
  195.3 2.4 copy-start.45
  195.3 2.4 copy-start.46
  195.3 36.8 %copy-start.24 = (f32[768]{0:T(1024)S(1)}, f32[768]{0:T(1024)}, u32[]{:S(2)}) copy-start(f32[768]{0:T(1024)} %convert_element_type.185) | copy-start | bytes 9220
  195.3 36.8 %copy-start.27 = (f32[512]{0:T(512)S(1)}, f32[512]{0:T(512)}, u32[]{:S(2)}) copy-start(f32[512]{0:T(512)} %copy-done.26) | copy-start | bytes 6148
  195.3 36.8 %copy-start.30 = (f32[512]{0:T(512)S(1)}, f32[512]{0:T(512)}, u32[]{:S(2)}) copy-start(f32[512]{0:T(512)} %copy-done.29) | copy-start | bytes 6148
  195.3 36.8 %copy-start.39 = (f32[768]{0:T(1024)S(1)}, f32[768]{0:T(1024)}, u32[]{:S(2)}) copy-start(f32[768]{0:T(1024)} %convert_element_type.186) | copy-start | bytes 9220
  197.6 81.4 %all-reduce.12.cloned.1.call-start = ((), (), s32[]{:S(2)}) async-start(), calls=%async_computation.6 | async-start | bytes 1572864 | tf_op jit(solution)/shard_map/psum | solution.py:151
  232.1 2.6 copy-start.14
  234.4 3.4 copy-start.53
  234.7 3.1 copy-start.52
  236.1 2.1 copy-start.49
  237.8 3.2 copy-start.3
  241.0 1.2 copy-start.50
  244.5 38.0 %copy-start.4 = (f32[512,768]{1,0:T(8,128)S(1)}, f32[512,768]{1,0:T(8,128)}, u32[]{:S(2)}) copy-start(f32[512,768]{1,0:T(8,128)} %copy-done.3) | copy-start | bytes 4718596
  244.5 38.0 %copy-start.9 = (bf16[512,768]{1,0:T(8,128)(2,1)S(1)}, bf16[512,768]{1,0:T(8,128)(2,1)}, u32[]{:S(2)}) copy-start(bf16[512,768]{1,0:T(8,128)(2,1)} %all-reduce.8.cloned.1.call-done) | copy-start | bytes 2359300
  244.5 147.7 %reduce-scatter.3.cloned.1.call-start = ((), (), s32[]{:S(2)}) async-start(), calls=%async_computation.7 | async-start | bytes 1966080 | tf_op jit(solution)/shard_map/reduce_scatter | solution.py:180
  279.0 3.6 copy-start.15
  282.6 2.5 copy-start.17
  283.9 1.1 copy-start.6
  356.8 1.4 copy-start.5
  356.8 72.0 %reduce-scatter.5.cloned.1.call-start = ((), (), s32[]{:S(2)}) async-start(), calls=%async_computation.8 | async-start | bytes 1966080 | tf_op jit(solution)/shard_map/reduce_scatter | solution.py:183
  357.4 5.9 copy-start.10
  357.4 5.9 copy-start.25
  357.4 5.9 copy-start.28
  357.4 5.9 copy-start.31
  357.4 142.0 %all-reduce.14.cloned.1.call-start = ((), (), s32[]{:S(2)}) async-start(), calls=%async_computation.9 | async-start | bytes 1572864 | tf_op jit(solution)/shard_map/psum | solution.py:199
  358.2 5.2 copy-start.40
  358.2 5.2 copy-start.51
  363.4 3.9 copy-start.22
  367.2 1.8 copy-start.7
  367.2 1.8 copy-start.13
  370.5 58.3 %copy-start.21 = (bf16[768,384]{1,0:T(8,128)(2,1)S(1)}, bf16[768,384]{1,0:T(8,128)(2,1)}, u32[]{:S(2)}) copy-start(bf16[768,384]{1,0:T(8,128)(2,1)} %param.26) | copy-start | bytes 1769476
  432.3 1.8 copy-start.11
  432.4 3.3 copy-start.18
  432.4 300.7 %all-reduce.16.cloned.1.call-start = ((), (), s32[]{:S(2)}) async-start(), calls=%async_computation.10 | async-start | bytes 28311552 | tf_op jit(solution)/shard_map/psum | solution.py:216
  437.1 0.7 copy-start.33
  437.2 0.7 copy-start.34
  437.2 0.7 copy-start.35
  437.2 0.7 copy-start.36
  437.2 0.7 copy-start.37
  437.2 0.7 copy-start.42
  733.0 5.5 copy-start.20
  735.8 4.1 copy-start.19
  739.9 6.5 slice-start
  741.0 5.5 slice-start.1
  746.5 3.4 copy-start.1
  (1 other events, 0.7 us)
Sparse Core Ops, SparseCore 0:
  23.2 59.2 all-gather.2
  147.6 34.8 all-reduce.7
  197.8 34.3 all-reduce.9
  244.6 34.3 all-reduce.11
  356.9 35.2 reduce-scatter.2
  394.5 34.2 reduce-scatter.4
  432.5 33.2 all-reduce.13
  472.1 260.9 all-reduce.15
